TPU v7x, 256 devices: a whole 4x4x8 slice. The times are simulated.
256 devices in a mesh: code: 32 (over y, z), dp: 8 (over x, core).
Axes of the slice: x: 4, y: 4, z: 8, core: 2. Of those that a mesh axis runs over, the one named last changes fastest.
Arguments:
- codebook: bfloat16 [262144, 768], P(('code', 'dp')), may hold values from -6 to 6
- weight_in: bfloat16 [768, 1024], replicated, may hold values from -0.21875 to 0.21875
- bias_in: float32 [1024], replicated, may hold values from -3 to 3
- weight_out: bfloat16 [1024, 256], replicated, may hold values from -0.1875 to 0.1875
- bias_out: float32 [256], replicated, may hold values from -3 to 3
- latents: float32 [262144, 256], P(('code', 'dp')), may hold values from -6 to 6
- cotangent: float32 [262144, 256], P(('code', 'dp')), may hold values from -6 to 6
- code_owner: int32 [262144, 1], P(('code', 'dp')), may hold values from 0 to 255; in each aligned block of 1024 rows (0 to 1023, 1024 to 2047, ...) at most 8 rows name the same one
- code_row: int32 [262144], P(('code', 'dp')), may hold values from 0 to 1023
Outputs:
- latent_grad: float32 [262144, 256], P(('code', 'dp'))
- grad_weight_in: float32 [768, 1024], replicated
- grad_bias_in: float32 [1024], replicated
- grad_weight_out: float32 [1024, 256], replicated
- grad_bias_out: float32 [256], replicated
Inputs may be any that keep to these rules, and one draw needn't show every extreme that they name: In the rows of one device no owner is named by more than 8 rows, a bound that some block reaches; a latent's code is code_owner * 1024 + code_row.
All inputs are finite; a program needn't handle non-finite values.
Results may differ from a plain program's by a relative error of at most 0.0023.
Values sent between devices are 32-bit elements; how exact they have to be, the bound alone decides.
A program may use at most 128 MiB of HBM per device.

v0:
```python
import jax
import jax.numpy as jnp
from jax import lax
from jax.sharding import PartitionSpec as P

scale_gelu = 0.7978845608028654
cubic_term = 0.044715


def in_blocks(array, dim, size):
    before, after = (array.shape[:dim], array.shape[dim + 1 :])
    return jnp.moveaxis(array.reshape(*before, size, -1, *after), dim, 0)


def in_order(tiles, dim):
    shape = list(tiles.shape[1:])
    shape[dim] *= tiles.shape[0]
    return jnp.moveaxis(tiles, 0, dim).reshape(shape)


def exchange_both(array, axis, axes, splits, concats):
    sizes = [lax.axis_size(a) for a in axes]
    tiles = in_blocks(array, splits[0], sizes[0])
    tiles = jnp.moveaxis(in_blocks(tiles, splits[1] + 1, sizes[1]), 0, 1)
    inside = tiles.shape[2:]
    tiles = tiles.reshape(-1, *inside)
    tiles = lax.all_to_all(tiles, axis, split_axis=0, concat_axis=0, tiled=True)
    tiles = in_order(tiles.reshape(*sizes, *inside), concats[0] + 1)
    return in_order(tiles, concats[1])


def gelu_value(x):
    inner = scale_gelu * (x + cubic_term * x * x * x)
    return 0.5 * x * (1.0 + jnp.tanh(inner))


def gelu_slope(x):
    tangent = jnp.tanh(scale_gelu * (x + cubic_term * x * x * x))
    return 0.5 * (1.0 + tangent) + 0.5 * x * (1.0 - tangent * tangent) * scale_gelu * (
        1.0 + 3.0 * cubic_term * x * x
    )


def per_device(
    codebook, weight_in, bias_in, weight_out, bias_out, latents, cotangent, code_owner, code_row
):
    preact = jnp.dot(codebook, weight_in, preferred_element_type=jnp.float32) + bias_in
    hidden = gelu_value(preact).astype(jnp.bfloat16)
    projected = jnp.dot(hidden, weight_out, preferred_element_type=jnp.float32) + bias_out
    n_code = lax.axis_size("code")
    n_data = lax.axis_size("dp")
    devices = n_code * n_data
    owners = code_owner[:, 0]
    count = owners.shape[0]
    width = latents.shape[1]
    capacity = max(2, 2 * count // devices)
    position = jnp.arange(count, dtype=jnp.int32)
    same = (owners[:, None] == owners[None, :]) & (position[None, :] < position[:, None])
    ranks = jnp.sum(same.astype(jnp.int32), axis=1)
    slots = owners * capacity + ranks
    wanted = jnp.full((devices * capacity,), -1, jnp.int32).at[slots].set(code_row)
    wanted = exchange_both(
        wanted.reshape(n_code, n_data, capacity), ("code", "dp"), ("code", "dp"), (0, 1), (0, 1)
    )
    valid = wanted >= 0
    row_ids = jnp.maximum(wanted, 0).reshape(-1)
    picked = jnp.take(projected, row_ids, axis=0).reshape(n_code, n_data, capacity, width)
    picked = jnp.where(valid[..., None], picked, 0.0)
    answers = exchange_both(picked, ("code", "dp"), ("code", "dp"), (0, 1), (0, 1))
    chosen = jnp.take(answers.reshape(devices * capacity, width), slots, axis=0)
    residual = chosen - latents
    latent_grad = cotangent - 0.25 * residual
    outgoing = (
        jnp.zeros((devices * capacity, width), jnp.float32).at[slots].set(cotangent + residual)
    )
    incoming = exchange_both(
        outgoing.reshape(n_code, n_data, capacity, width),
        ("code", "dp"),
        ("code", "dp"),
        (0, 1),
        (0, 1),
    )
    code_grad = jax.ops.segment_sum(
        incoming.reshape(devices * capacity, width), row_ids, num_segments=projected.shape[0]
    )
    code_low = code_grad.astype(jnp.bfloat16)
    gw_out = lax.dot_general(
        hidden, code_low, (((0,), (0,)), ((), ())), preferred_element_type=jnp.float32
    )
    back = lax.dot_general(
        code_low, weight_out, (((1,), (1,)), ((), ())), preferred_element_type=jnp.float32
    )
    preact_grad = (back * gelu_slope(preact)).astype(jnp.bfloat16)
    gb_in = jnp.sum(preact_grad.astype(jnp.float32), axis=0)
    gw_in = lax.dot_general(
        codebook, preact_grad, (((0,), (0,)), ((), ())), preferred_element_type=jnp.float32
    )
    gb_out = jnp.sum(code_grad, axis=0)
    gw_in, gb_in, gw_out, gb_out = lax.psum((gw_in, gb_in, gw_out, gb_out), ("code", "dp"))
    return (latent_grad, gw_in, gb_in, gw_out, gb_out)


def solution(mesh):
    placed = (
        P(("code", "dp"), None),
        P(),
        P(),
        P(),
        P(),
        P(("code", "dp"), None),
        P(("code", "dp"), None),
        P(("code", "dp"), None),
        P(("code", "dp")),
    )
    return jax.shard_map(
        per_device,
        mesh=mesh,
        in_specs=placed,
        out_specs=(P(("code", "dp"), None), P(), P(), P(), P()),
        check_vma=False,
    )
```

profile of v0, /device:TPU:97, one launch (start us, length us, event | category | flops | bytes accessed | tf_op | source)
XLA Modules:
  0.0 492.3 jit_solution(8340644630260382695)
XLA Ops:
  7.2 1.3 convert_reduce_fusion.1
  9.2 4.5 scatter_custom_fusion
  13.7 0.8 reshape_transpose_transpose_reshape_reshape_reshape.6
  14.5 14.3 %all-to-all-start = ((s32[256,1,1,8]{3,2,1,0:T(1,128)}), s32[256,1,1,8]{3,2,1,0:T(1,128)S(1)}, u32[]{:S(2)}, u32[]{:S(2)}) async-start(s32[256,1,1,8]{3,2,1,0:T(1,128)} %bitcast.3), calls=%async_computation | async-start | bytes 262144 | tf_op jit(solution)/shard_map/all_to_all | solution.py:27
  28.8 5.9 %multiply_convert_fusion = (bf16[1024,1024]{1,0:T(8,128)(2,1)S(1)}, f32[1024,1024]{1,0:T(8,128)}) fusion(f32[1024]{0:T(1024)} %param.11, bf16[1024,768]{1,0:T(8,128)(2,1)S(1)} %copy-done, bf16[768,1024]{1,0:T(8,128)(2,1)} %param.10), kind=kOutput, calls=%fused_computation.15 | convolution fusion | flops 1621098496 | bytes 9441280 | tf_op jit(solution)/shard_map/dot_general | solution.py:47
  34.7 1.3 copy-done.6
  36.8 1.8 all-to-all-done
  39.5 8.6 %gather_fusion = f32[2048,256]{1,0:T(8,128)} fusion(f32[1024,256]{1,0:T(8,128)S(1)} %convolution_add_fusion, s32[2048]{0:T(1024)S(1)} %broadcast_clamp_fusion), kind=kCustom, calls=%fused_computation | custom fusion | bytes 4202496 | tf_op jit(solution)/shard_map/jit(_take)/gather | solution.py:67
  48.1 4.2 fusion.10
  52.3 12.9 %all-to-all-start.1 = ((f32[256,1,1,8,256]{4,3,2,1,0:T(8,128)}), f32[256,1,1,8,256]{4,3,2,1,0:T(8,128)}, u32[]{:S(2)}, u32[]{:S(2)}) async-start(f32[256,1,1,8,256]{4,3,2,1,0:T(8,128)} %fusion.10), calls=%async_computation.1 | async-start | bytes 4194304 | tf_op jit(solution)/shard_map/all_to_all | solution.py:27
  65.2 49.4 %all-to-all-done.1 = f32[256,1,1,8,256]{4,3,2,1,0:T(8,128)} async-done(((f32[256,1,1,8,256]{4,3,2,1,0:T(8,128)}), f32[256,1,1,8,256]{4,3,2,1,0:T(8,128)}, u32[]{:S(2)}, u32[]{:S(2)}) %all-to-all-start.1) | async-done | bytes 2097184 | tf_op jit(solution)/shard_map/all_to_all | solution.py:27
  114.6 5.1 %gather_fusion.1 = f32[1024,256]{1,0:T(8,128)S(1)} fusion(f32[2048,256]{1,0:T(8,128)} %bitcast.22, s32[1024]{0:T(1024)S(1)} %broadcast_clamp_fusion.1), kind=kCustom, calls=%fused_computation.1 | custom fusion | bytes 2101248 | tf_op jit(solution)/shard_map/jit(_take)/gather | solution.py:70
  119.7 7.5 %scatter_custom_fusion.1 = f32[2048,256]{1,0:T(8,128)} fusion(s32[1024]{0:T(1024)S(1)} %bitcast.77, f32[1024,256]{1,0:T(8,128)} %param.15, f32[]{:T(128)} %constant.32.clone.1, f32[1024,256]{1,0:T(8,128)} %param.14, f32[1024,256]{1,0:T(8,128)S(1)} %gather_fusion.1, f32[]{:T(128)} %constant.31.clone.1, pred[1024]{0:T(1024)(128)(4,1)S(1)} %get-tuple-element.39), kind=kCustom, calls=%fused_computation.25 | custom fusion | flops 786432 | bytes 5243912 | tf_op jit(solution)/shard_map/scatter | solution.py:74
  127.1 60.8 %all_to_all.15 = f32[256,1,1,8,256]{4,3,2,1,0:T(8,128)} all-to-all(f32[256,1,1,8,256]{4,3,2,1,0:T(8,128)} %bitcast.70), channel_id=1, replica_groups=mesh['code'=32,'dp'=8] {'code','dp'}, dimensions={0} | all-to-all | bytes 4194304 | tf_op jit(solution)/shard_map/all_to_all | solution.py:27
  187.9 13.1 %scatter_custom_fusion.2 = f32[1024,256]{1,0:T(8,128)} fusion(s32[2048]{0:T(1024)S(1)} %reshape.110, f32[256,1,1,8,256]{4,3,2,1,0:T(8,128)} %all_to_all.15, f32[]{:T(128)} %constant.32.clone.1), kind=kCustom, calls=%fused_computation.19 | custom fusion | flops 524288 | bytes 3145732 | tf_op jit(solution)/shard_map/scatter-add | solution.py:83
  201.0 3.8 fusion.15
  204.8 3.2 convert_reduce_fusion
  208.0 3.5 convolution_bitcast_fusion
  211.6 2.8 multiply_subtract_fusion
  214.3 1.4 reduce_sum.32
  215.7 74.4 %all-reduce = (f32[1024]{0:T(1024)}, f32[256]{0:T(256)}) all-reduce(f32[1024]{0:T(1024)S(1)} %get-tuple-element.43, f32[256]{0:T(256)S(1)} %reduce_sum.32), channel_id=1, replica_groups=mesh['code'=32,'dp'=8] {'code','dp'}, use_global_device_ids=true, to_apply=%region_6.7 | all-reduce | flops 1280 | bytes 10240 | tf_op jit(solution)/shard_map/psum | solution.py:99
  290.2 190.7 %all-reduce.4.cloned.1.call-done = (f32[768,1024]{0,1:T(8,128)}, f32[1024,256]{1,0:T(8,128)}) async-done(((f32[768,1024]{0,1:T(8,128)}, f32[1024,256]{1,0:T(8,128)}), (f32[768,1024]{0,1:T(8,128)}, f32[1024,256]{1,0:T(8,128)})) %all-reduce.4.cloned.1.call-update) | async-done | bytes 4194320 | tf_op jit(solution)/shard_map/psum | solution.py:99
  480.8 3.6 copy.33
  484.5 1.0 copy.37
  (28 shorter events, 2.4 us)
Async XLA Ops:
  7.2 21.6 %copy-start = (bf16[1024,768]{1,0:T(8,128)(2,1)S(1)}, bf16[1024,768]{1,0:T(8,128)(2,1)}, u32[]{:S(2)}) copy-start(bf16[1024,768]{1,0:T(8,128)(2,1)} %param.9) | copy-start | bytes 4718596
  14.5 24.1 %all-to-all-start = ((s32[256,1,1,8]{3,2,1,0:T(1,128)}), s32[256,1,1,8]{3,2,1,0:T(1,128)S(1)}, u32[]{:S(2)}, u32[]{:S(2)}) async-start(s32[256,1,1,8]{3,2,1,0:T(1,128)} %bitcast.3), calls=%async_computation | async-start | bytes 262144 | tf_op jit(solution)/shard_map/all_to_all | solution.py:27
  28.8 7.3 %copy-start.3 = (bf16[1024,256]{1,0:T(8,128)(2,1)S(1)}, bf16[1024,256]{1,0:T(8,128)(2,1)}, u32[]{:S(2)}) copy-start(bf16[1024,256]{1,0:T(8,128)(2,1)} %param.12) | copy-start | bytes 1572868
  28.8 7.2 %copy-start.5 = (f32[256]{0:T(256)S(1)}, f32[256]{0:T(256)}, u32[]{:S(2)}) copy-start(f32[256]{0:T(256)} %param.13) | copy-start | bytes 3076
  34.7 1.3 copy-start.6
  52.3 62.3 %all-to-all-start.1 = ((f32[256,1,1,8,256]{4,3,2,1,0:T(8,128)}), f32[256,1,1,8,256]{4,3,2,1,0:T(8,128)}, u32[]{:S(2)}, u32[]{:S(2)}) async-start(f32[256,1,1,8,256]{4,3,2,1,0:T(8,128)} %fusion.10), calls=%async_computation.1 | async-start | bytes 4194304 | tf_op jit(solution)/shard_map/all_to_all | solution.py:27
  65.2 415.6 %all-reduce.4.cloned.1.call-start = ((), (), s32[]{:S(2)}) async-start(), calls=%async_computation.3 | async-start | bytes 8388608 | tf_op jit(solution)/shard_map/psum | solution.py:99
  201.0 3.8 copy-start.1
  201.0 3.8 copy-start.4
  201.0 3.8 copy-start.7
  480.8 3.6 copy-start.2
Sparse Core Ops, SparseCore 0:
  211.7 269.0 all-reduce.3
where the time goes:
time: 493 us; the launch traced here: 492 us
  waiting for transfers between devices  242 us (49%)
  blocking collectives  135 us (27%)
  other arithmetic  31.3 us (6%)
  starting transfers between devices  27.2 us (6%)
  local copies, waits for them, and re-layouts  25.3 us (5%)
  matrix products  17.1 us (3%)
  between operations  14.2 us (3%)
    psum x1, waiting for transfers between devices, per_device(): lax.psum((gw_in, gb_in, gw_out, gb_out), ('code', 'dp'))  191 us
    psum x1, blocking collectives, per_device(): lax.psum((gw_in, gb_in, gw_out, gb_out), ('code', 'dp'))  74.4 us
    all_to_all x1, blocking collectives, exchange_both(): tiles = lax.all_to_all(tiles, axis, split_axis=0, concat_axis=0, tiled=True)  60.8 us
    all_to_all x2, waiting for transfers between devices, exchange_both(): tiles = lax.all_to_all(tiles, axis, split_axis=0, concat_axis=0, tiled=True)  51.2 us
    all_to_all x2, starting transfers between devices, exchange_both(): tiles = lax.all_to_all(tiles, axis, split_axis=0, concat_axis=0, tiled=True)  27.2 us
    scatter-add x1, other arithmetic, per_device(): jax.ops.segment_sum(incoming.reshape(devices * capacity, width), row_ids,...  13.1 us
  transfers between devices with their start and end apart: 3, of which 3 were waited for; matrix products, arithmetic and copies ran while one was open for 2% of the time, Pallas kernels for 0%

commit v1 on v0

--- a/solution.py
+++ b/solution.py
@@ -96,7 +96,9 @@
         codebook, preact_grad, (((0,), (0,)), ((), ())), preferred_element_type=jnp.float32
     )
     gb_out = jnp.sum(code_grad, axis=0)
-    gw_in, gb_in, gw_out, gb_out = lax.psum((gw_in, gb_in, gw_out, gb_out), ("code", "dp"))
+    gw_in, gb_in, gw_out, gb_out = jax.lax.psum(
+        jax.lax.psum((gw_in, gb_in, gw_out, gb_out), "dp"), "code"
+    )
     return (latent_grad, gw_in, gb_in, gw_out, gb_out)
 
 

time: 493 us -> 468 us (0.949)
  waiting for transfers between devices: 242 us -> 217 us
    psum x1 -> x2, waiting for transfers between devices: 191 us -> 166 us  [the longest x1 93.2 us: per_device(): jax.lax.psum(jax.lax.psum((gw_in, gb_in, gw_out, gb_out), 'dp'), 'code')]
    psum x1 -> x2, blocking collectives: 74.4 us -> 70.5 us  [the longest x1 56.2 us: per_device(): jax.lax.psum(jax.lax.psum((gw_in, gb_in, gw_out, gb_out), 'dp'), 'code')]
  transfers between devices with their start and end apart: 3 -> 4, of which waited for: 3 -> 4; matrix products, arithmetic and copies ran while one was open for 2% -> 2% of each run, Pallas kernels for 0% -> 0%
where the time goes in v1:
time: 468 us; the launch traced here: 464 us
  waiting for transfers between devices  217 us (46%)
  blocking collectives  131 us (28%)
  other arithmetic  31.3 us (7%)
  starting transfers between devices  27.3 us (6%)
  local copies, waits for them, and re-layouts  25.3 us (5%)
  matrix products  17.1 us (4%)
  between operations  14.2 us (3%)
    psum x1, waiting for transfers between devices, per_device(): jax.lax.psum(jax.lax.psum((gw_in, gb_in, gw_out, gb_out), 'dp'), 'code')  93.2 us
    psum x1, waiting for transfers between devices, per_device(): jax.lax.psum((gw_in, gb_in, gw_out, gb_out), 'dp')  72.9 us
    all_to_all x1, blocking collectives, exchange_both(): tiles = lax.all_to_all(tiles, axis, split_axis=0, concat_axis=0, tiled=True)  60.8 us
    psum x1, blocking collectives, per_device(): jax.lax.psum(jax.lax.psum((gw_in, gb_in, gw_out, gb_out), 'dp'), 'code')  56.2 us
    all_to_all x2, waiting for transfers between devices, exchange_both(): tiles = lax.all_to_all(tiles, axis, split_axis=0, concat_axis=0, tiled=True)  51.2 us
    all_to_all x2, starting transfers between devices, exchange_both(): tiles = lax.all_to_all(tiles, axis, split_axis=0, concat_axis=0, tiled=True)  27.2 us
    psum x1, blocking collectives, per_device(): jax.lax.psum((gw_in, gb_in, gw_out, gb_out), 'dp')  14.3 us
    scatter-add x1, other arithmetic, per_device(): jax.ops.segment_sum(incoming.reshape(devices * capacity, width), row_ids,...  13.1 us
  transfers between devices with their start and end apart: 4, of which 4 were waited for; matrix products, arithmetic and copies ran while one was open for 2% of the time, Pallas kernels for 0%

profile of v1, /device:TPU:97, one launch (start us, length us, event | category | flops | bytes accessed | tf_op | source)
XLA Modules:
  0.0 463.7 jit_solution(13004589228749882816)
XLA Ops:
  7.2 1.3 convert_reduce_fusion.1
  9.2 4.5 scatter_custom_fusion
  14.5 14.3 %all-to-all-start = ((s32[256,1,1,8]{3,2,1,0:T(1,128)}), s32[256,1,1,8]{3,2,1,0:T(1,128)S(1)}, u32[]{:S(2)}, u32[]{:S(2)}) async-start(s32[256,1,1,8]{3,2,1,0:T(1,128)} %bitcast.3), calls=%async_computation | async-start | bytes 262144 | tf_op jit(solution)/shard_map/all_to_all | solution.py:27
  28.8 5.9 %multiply_convert_fusion = (bf16[1024,1024]{1,0:T(8,128)(2,1)S(1)}, f32[1024,1024]{1,0:T(8,128)}) fusion(f32[1024]{0:T(1024)} %param.11, bf16[1024,768]{1,0:T(8,128)(2,1)S(1)} %copy-done, bf16[768,1024]{1,0:T(8,128)(2,1)} %param.10), kind=kOutput, calls=%fused_computation.15 | convolution fusion | flops 1621098496 | bytes 9441280 | tf_op jit(solution)/shard_map/dot_general | solution.py:47
  34.7 1.3 copy-done.6
  36.8 1.8 all-to-all-done
  39.5 8.6 %gather_fusion = f32[2048,256]{1,0:T(8,128)} fusion(f32[1024,256]{1,0:T(8,128)S(1)} %convolution_add_fusion, s32[2048]{0:T(1024)S(1)} %broadcast_clamp_fusion), kind=kCustom, calls=%fused_computation | custom fusion | bytes 4202496 | tf_op jit(solution)/shard_map/jit(_take)/gather | solution.py:67
  48.1 4.2 fusion.10
  52.3 12.9 %all-to-all-start.1 = ((f32[256,1,1,8,256]{4,3,2,1,0:T(8,128)}), f32[256,1,1,8,256]{4,3,2,1,0:T(8,128)}, u32[]{:S(2)}, u32[]{:S(2)}) async-start(f32[256,1,1,8,256]{4,3,2,1,0:T(8,128)} %fusion.10), calls=%async_computation.1 | async-start | bytes 4194304 | tf_op jit(solution)/shard_map/all_to_all | solution.py:27
  65.2 49.4 %all-to-all-done.1 = f32[256,1,1,8,256]{4,3,2,1,0:T(8,128)} async-done(((f32[256,1,1,8,256]{4,3,2,1,0:T(8,128)}), f32[256,1,1,8,256]{4,3,2,1,0:T(8,128)}, u32[]{:S(2)}, u32[]{:S(2)}) %all-to-all-start.1) | async-done | bytes 2097184 | tf_op jit(solution)/shard_map/all_to_all | solution.py:27
  114.6 5.1 %gather_fusion.1 = f32[1024,256]{1,0:T(8,128)S(1)} fusion(f32[2048,256]{1,0:T(8,128)} %bitcast.22, s32[1024]{0:T(1024)S(1)} %broadcast_clamp_fusion.1), kind=kCustom, calls=%fused_computation.1 | custom fusion | bytes 2101248 | tf_op jit(solution)/shard_map/jit(_take)/gather | solution.py:70
  119.7 7.5 %scatter_custom_fusion.1 = f32[2048,256]{1,0:T(8,128)} fusion(s32[1024]{0:T(1024)S(1)} %bitcast.77, f32[1024,256]{1,0:T(8,128)} %param.15, f32[]{:T(128)} %constant.32.clone.1, f32[1024,256]{1,0:T(8,128)} %param.14, f32[1024,256]{1,0:T(8,128)S(1)} %gather_fusion.1, f32[]{:T(128)} %constant.31.clone.1, pred[1024]{0:T(1024)(128)(4,1)S(1)} %get-tuple-element.43), kind=kCustom, calls=%fused_computation.25 | custom fusion | flops 786432 | bytes 5243912 | tf_op jit(solution)/shard_map/scatter | solution.py:74
  127.1 60.8 %all_to_all.15 = f32[256,1,1,8,256]{4,3,2,1,0:T(8,128)} all-to-all(f32[256,1,1,8,256]{4,3,2,1,0:T(8,128)} %bitcast.70), channel_id=1, replica_groups=mesh['code'=32,'dp'=8] {'code','dp'}, dimensions={0} | all-to-all | bytes 4194304 | tf_op jit(solution)/shard_map/all_to_all | solution.py:27
  187.9 13.1 %scatter_custom_fusion.2 = f32[1024,256]{1,0:T(8,128)} fusion(s32[2048]{0:T(1024)S(1)} %reshape.110, f32[256,1,1,8,256]{4,3,2,1,0:T(8,128)} %all_to_all.15, f32[]{:T(128)} %constant.32.clone.1), kind=kCustom, calls=%fused_computation.19 | custom fusion | flops 524288 | bytes 3145732 | tf_op jit(solution)/shard_map/scatter-add | solution.py:83
  201.0 3.7 fusion.15
  204.7 3.2 convert_reduce_fusion
  208.0 3.6 convolution_bitcast_fusion
  211.6 72.9 %all-reduce.9.cloned.1.call-done = (f32[768,1024]{0,1:T(8,128)}, f32[1024,256]{1,0:T(8,128)}) async-done(((f32[768,1024]{0,1:T(8,128)}, f32[1024,256]{1,0:T(8,128)}), (f32[768,1024]{0,1:T(8,128)}, f32[1024,256]{1,0:T(8,128)})) %all-reduce.9.cloned.1.call-update) | async-done | bytes 4194320 | tf_op jit(solution)/shard_map/psum | solution.py:100
  284.5 2.8 multiply_subtract_fusion
  287.3 1.4 reduce_sum.32
  288.6 14.3 %all-reduce.2 = (f32[1024]{0:T(1024)S(1)}, f32[256]{0:T(256)S(1)}) all-reduce(f32[1024]{0:T(1024)S(1)} %get-tuple-element.47, f32[256]{0:T(256)S(1)} %reduce_sum.32), channel_id=1, replica_groups=mesh['code'=32,'dp'=8] {'dp'}, use_global_device_ids=true, to_apply=%region_7.8 | all-reduce | flops 1280 | bytes 10240 | tf_op jit(solution)/shard_map/psum | solution.py:100
  302.9 56.2 %all-reduce = (f32[1024]{0:T(1024)}, f32[256]{0:T(256)}) all-reduce(f32[1024]{0:T(1024)S(1)} %get-tuple-element.39, f32[256]{0:T(256)S(1)} %get-tuple-element.40), channel_id=1, replica_groups=mesh['code'=32,'dp'=8] {'code'}, use_global_device_ids=true, to_apply=%region_8.9 | all-reduce | flops 1280 | bytes 10240 | tf_op jit(solution)/shard_map/psum | solution.py:99
  359.1 93.2 %all-reduce.7.cloned.1.call-done = (f32[768,1024]{0,1:T(8,128)}, f32[1024,256]{1,0:T(8,128)}) async-done(((f32[768,1024]{0,1:T(8,128)}, f32[1024,256]{1,0:T(8,128)}), (f32[768,1024]{0,1:T(8,128)}, f32[1024,256]{1,0:T(8,128)})) %all-reduce.7.cloned.1.call-update) | async-done | bytes 4194320 | tf_op jit(solution)/shard_map/psum | solution.py:99
  452.3 3.6 copy.33
  (32 shorter events, 4.1 us)
Async XLA Ops:
  7.2 21.6 %copy-start = (bf16[1024,768]{1,0:T(8,128)(2,1)S(1)}, bf16[1024,768]{1,0:T(8,128)(2,1)}, u32[]{:S(2)}) copy-start(bf16[1024,768]{1,0:T(8,128)(2,1)} %param.9) | copy-start | bytes 4718596
  14.5 24.1 %all-to-all-start = ((s32[256,1,1,8]{3,2,1,0:T(1,128)}), s32[256,1,1,8]{3,2,1,0:T(1,128)S(1)}, u32[]{:S(2)}, u32[]{:S(2)}) async-start(s32[256,1,1,8]{3,2,1,0:T(1,128)} %bitcast.3), calls=%async_computation | async-start | bytes 262144 | tf_op jit(solution)/shard_map/all_to_all | solution.py:27
  28.8 7.3 %copy-start.3 = (bf16[1024,256]{1,0:T(8,128)(2,1)S(1)}, bf16[1024,256]{1,0:T(8,128)(2,1)}, u32[]{:S(2)}) copy-start(bf16[1024,256]{1,0:T(8,128)(2,1)} %param.12) | copy-start | bytes 1572868
  28.8 7.2 %copy-start.5 = (f32[256]{0:T(256)S(1)}, f32[256]{0:T(256)}, u32[]{:S(2)}) copy-start(f32[256]{0:T(256)} %param.13) | copy-start | bytes 3076
  34.7 1.3 copy-start.6
  52.3 62.3 %all-to-all-start.1 = ((f32[256,1,1,8,256]{4,3,2,1,0:T(8,128)}), f32[256,1,1,8,256]{4,3,2,1,0:T(8,128)}, u32[]{:S(2)}, u32[]{:S(2)}) async-start(f32[256,1,1,8,256]{4,3,2,1,0:T(8,128)} %fusion.10), calls=%async_computation.1 | async-start | bytes 4194304 | tf_op jit(solution)/shard_map/all_to_all | solution.py:27
  65.2 219.3 %all-reduce.9.cloned.1.call-start = ((), (), s32[]{:S(2)}) async-start(), calls=%async_computation.4 | async-start | bytes 8388608 | tf_op jit(solution)/shard_map/psum | solution.py:100
  201.0 3.7 copy-start.1
  201.0 3.7 copy-start.4
  201.0 3.7 copy-start.7
  211.6 240.7 %all-reduce.7.cloned.1.call-start = ((), (), s32[]{:S(2)}) async-start(), calls=%async_computation.3 | async-start | bytes 8388608 | tf_op jit(solution)/shard_map/psum | solution.py:99
  452.3 3.6 copy-start.2
Sparse Core Ops, SparseCore 0:
  211.7 72.7 all-reduce.8
  288.2 164.0 all-reduce.6
